TPU v7x, 512 devices: a whole 4x8x8 slice. The times are simulated.
512 devices in a mesh: freq: 128 (over z, y, core), panel: 4 (over x).
Axes of the slice: x: 4, y: 8, z: 8, core: 2. Of those that a mesh axis runs over, the one named last changes fastest.
Arguments:
- wave: bfloat16 [2, 128, 1600, 1600], P(None, 'freq', 'panel'), may hold values from -0.15625 to 0.15625
- observed: float32 [4, 6400, 512], P('panel', 'freq'), may hold values from -25 to 25
Outputs:
- solution: float32 [25600, 512], P('freq')
All inputs are finite; a program needn't handle non-finite values.
Results may differ from a plain program's by a relative error of at most 0.0085.
Values may be sent and summed in bfloat16 or wider, within the bound.
A program may use at most 64 MiB of HBM per device.

v0:
```python
import math
import jax
import jax.numpy as jnp
from jax import lax
from jax.sharding import PartitionSpec as P

VS = 16
ITERS = 3
SCALE = 0.5
precise = lax.Precision.HIGHEST
epsilon = 1e-06


def transform_tables(freq_total, samples):
    freq_index = lax.broadcasted_iota(jnp.int32, (freq_total, samples), 0) + 1
    time_index = lax.broadcasted_iota(jnp.int32, (freq_total, samples), 1)
    phases = (freq_index * time_index % samples).astype(jnp.float32) * (2.0 * math.pi / samples)
    factor = math.sqrt(2.0 / samples)
    return jnp.stack([factor * jnp.cos(phases), -factor * jnp.sin(phases)])


def two_parts(field):
    high = lax.reduce_precision(field, 8, 7)
    return jnp.concatenate([high, field - high]).astype(jnp.bfloat16)


def forward_product(model, wave):
    rows = two_parts(model.reshape(2 * VS, -1))

    def product_of(right):
        both = lax.dot_general(
            rows, right, (((1,), (1,)), ((), ())), preferred_element_type=jnp.float32
        )
        return both[: 2 * VS] + both[2 * VS :]

    by_real, by_imag = (product_of(wave[0]), product_of(wave[1]))
    return SCALE * jnp.stack([by_real[:VS] - by_imag[VS:], by_imag[:VS] + by_real[VS:]])


def adjoint_product(rows, wave):

    def product_of(right):
        both = jnp.dot(rows, right, preferred_element_type=jnp.float32)
        return both if rows.shape[0] == 2 * VS else both[: 2 * VS] + both[2 * VS :]

    by_real, by_imag = (product_of(wave[0]), product_of(wave[1]))
    return SCALE * jnp.stack([by_real[:VS] + by_imag[VS:], by_real[VS:] - by_imag[:VS]])


def iterate_weights(data_square, moments):
    model_norms = [jnp.sqrt(moments[2 * k]) for k in range(ITERS)]
    data_norms = [jnp.sqrt(data_square)] + [jnp.sqrt(moments[2 * k + 1]) for k in range(ITERS)]

    def ratio(top, bottom):
        return jnp.where(bottom > 0, top / jnp.where(bottom > 0, bottom, 1.0), 0.0)

    model_gram = [
        [ratio(ratio(moments[i + j], model_norms[i]), model_norms[j]) for j in range(ITERS)]
        for i in range(ITERS)
    ]

    def data_inner(i, j):
        low, high = (min(i, j), max(i, j))
        if high == 0:
            return data_square
        if low == 0:
            return moments[high - 1]
        return moments[low + high - 1]

    data_gram = [
        [ratio(ratio(data_inner(i, j), data_norms[i]), data_norms[j]) for j in range(ITERS + 1)]
        for i in range(ITERS + 1)
    ]

    def norm_of(weights, gram):
        total = 0.0
        for i in range(len(weights)):
            total += weights[i] * weights[i] * ratio(gram[i][i], gram[i][i])
            for j in range(i):
                total += 2.0 * weights[i] * weights[j] * gram[i][j]
        return jnp.sqrt(jnp.maximum(total, 0.0) + epsilon)

    up = [ratio(data_norms[k + 1], model_norms[k]) / SCALE for k in range(ITERS)]
    down = [ratio(model_norms[k], data_norms[k]) / SCALE for k in range(ITERS)]
    zero = jnp.zeros_like(data_square)
    beta = jnp.sqrt(data_square + epsilon)
    data_vector = [data_norms[0] / beta] + [zero] * ITERS
    model_vector = [data_vector[k] * down[k] for k in range(ITERS)]
    alpha = norm_of(model_vector, model_gram)
    model_vector = [weight / alpha for weight in model_vector]
    direction = model_vector
    solution = [zero] * ITERS
    phi_bar = beta
    rho_bar = alpha
    for step in range(ITERS):
        image = [zero] + [model_vector[k] * up[k] for k in range(ITERS)]
        data_vector = [new - alpha * old for new, old in zip(image, data_vector)]
        beta = norm_of(data_vector, data_gram)
        data_vector = [weight / beta for weight in data_vector]
        rho_new = jnp.sqrt(rho_bar * rho_bar + beta * beta)
        cosine = rho_bar / rho_new
        sine_part = beta / rho_new
        phi_value = cosine * phi_bar
        phi_bar = sine_part * phi_bar
        solution = [old + phi_value / rho_new * weight for old, weight in zip(solution, direction)]
        if step < ITERS - 1:
            image = [data_vector[k] * down[k] for k in range(ITERS)]
            model_vector = [new - beta * old for new, old in zip(image, model_vector)]
            alpha = norm_of(model_vector, model_gram)
            model_vector = [weight / alpha for weight in model_vector]
            theta = sine_part * alpha
            rho_bar = -cosine * alpha
            direction = [
                weight - theta / rho_new * old for weight, old in zip(model_vector, direction)
            ]
    return [ratio(weight, norm) for weight, norm in zip(solution, model_norms)]


def on_device(wave, observed):
    wave = wave[:, 0]
    panel_rows, sources = wave.shape[1:]
    blocks = lax.axis_size("freq")
    panels = lax.axis_size("panel")
    samples = observed.shape[2]
    table = transform_tables(blocks, samples)
    data = observed[0]

    def exchange(lines):
        return lax.all_to_all(lines, "freq", split_axis=0, concat_axis=0, tiled=True)

    lines = jnp.einsum("cft,rt->fcr", table, data, precision=precise).astype(jnp.bfloat16)
    moved_in = exchange(lines.reshape(-1)).reshape(blocks, 2, -1)
    rows = moved_in.transpose(1, 0, 2).reshape(2 * VS, panel_rows)
    bases, squares = ([], [jnp.sum(data * data)])
    for step in range(ITERS):
        model = lax.psum(adjoint_product(rows, wave), "panel")
        image = forward_product(model, wave)
        bases.append(model)
        squares += [jnp.sum(model * model) / panels, jnp.sum(image * image)]
        rows = two_parts(image.reshape(2 * VS, -1))
    squares = lax.psum(jnp.stack(squares), ("freq", "panel"))
    weights = iterate_weights(squares[0], [squares[1 + k] for k in range(2 * ITERS)])
    spectrum = sum((weight * basis for weight, basis in zip(weights, bases)))
    spectrum = spectrum.astype(jnp.bfloat16).reshape(2, blocks, -1)
    moved = exchange(spectrum.transpose(1, 0, 2).reshape(-1)).reshape(blocks, 2, -1)
    return jnp.einsum("jcr,cjt->rt", moved.astype(jnp.float32), table, precision=precise)


def solution(mesh):
    placed = (P(None, "freq", "panel", None), P("panel", "freq", None))
    return jax.shard_map(
        on_device, mesh=mesh, in_specs=placed, out_specs=P("freq", None), check_vma=False
    )
```

profile of v0, /device:TPU:1, one launch (start us, length us, event | category | flops | bytes accessed | tf_op | source)
XLA Modules:
  0.0 358.5 jit_solution(4462551454970142538)
XLA Ops:
  6.5 1.1 cosine_multiply_fusion
  7.7 1.5 fusion.24
  9.3 29.7 %all_to_all.18 = bf16[128,100,1]{1,2,0:T(2,128)(2,1)S(1)} all-to-all(bf16[128,100,1]{1,2,0:T(2,128)(2,1)S(1)} %copy.5), channel_id=1, replica_groups=mesh['freq'=128,'panel'=4] {'freq'}, dimensions={0} | all-to-all | bytes 51200 | tf_op jit(solution)/shard_map/all_to_all | solution.py:129
  39.4 1.7 fusion.10
  41.5 0.7 maximum_multiply_fusion
  42.3 42.4 %all-reduce.4.cloned.1.call-done = f32[2,16,1600]{2,1,0:T(8,128)} async-done(((f32[2,16,1600]{2,1,0:T(8,128)}), f32[2,16,1600]{2,1,0:T(8,128)}) %all-reduce.4.cloned.1.call-update) | async-done | bytes 204816 | tf_op jit(solution)/shard_map/psum | solution.py:136
  84.6 1.0 reduce-precision_convert_fusion.2
  85.6 0.5 fusion.20
  86.1 0.5 fusion.8
  86.7 0.6 multiply_reduce_fusion.4
  88.1 0.7 maximum_multiply_fusion.1
  88.9 0.7 fusion.47
  89.6 51.8 %all-reduce.6.cloned.1.call-done = f32[2,16,1600]{2,1,0:T(8,128)} async-done(((f32[2,16,1600]{2,1,0:T(8,128)}), f32[2,16,1600]{2,1,0:T(8,128)}) %all-reduce.6.cloned.1.call-update) | async-done | bytes 204816 | tf_op jit(solution)/shard_map/psum | solution.py:136
  141.4 1.0 reduce-precision_convert_fusion.1
  142.3 0.5 fusion.16
  142.9 0.5 fusion.4
  143.5 0.6 multiply_reduce_fusion.3
  144.9 0.7 maximum_multiply_fusion.2
  145.7 0.7 multiply_reduce_fusion.2
  146.9 1.7 multiply_reduce_fusion.1
  149.2 48.9 %all-reduce.8.cloned.1.call-done = f32[2,16,1600]{2,1,0:T(8,128)} async-done(((f32[2,16,1600]{2,1,0:T(8,128)}), f32[2,16,1600]{2,1,0:T(8,128)}) %all-reduce.8.cloned.1.call-update) | async-done | bytes 204816 | tf_op jit(solution)/shard_map/psum | solution.py:136
  198.1 1.0 reduce-precision_convert_fusion
  199.2 0.5 fusion.12
  200.3 0.7 multiply_reduce_fusion
  201.6 0.7 fusion.58
  202.3 2.6 stack.109
  204.9 99.4 %psum.31 = f32[7]{0:T(128)S(1)} all-reduce(f32[7]{0:T(128)S(1)} %stack.109), channel_id=1, replica_groups=mesh['freq'=128,'panel'=4] {'freq','panel'}, use_global_device_ids=true, to_apply=%region_10.11 | all-reduce | flops 7 | bytes 56 | tf_op jit(solution)/shard_map/psum | solution.py:141
  304.2 0.7 fusion.77
  324.2 1.1 add_convert_fusion
  326.3 1.4 reduce
  327.9 22.6 %all_to_all.19 = bf16[128,2,200]{2,1,0:T(2,128)(2,1)S(1)} all-to-all(bf16[128,2,200]{2,1,0:T(2,128)(2,1)S(1)} %reshape.144), channel_id=1, replica_groups=mesh['freq'=128,'panel'=4] {'freq'}, dimensions={0} | all-to-all | bytes 204800 | tf_op jit(solution)/shard_map/all_to_all | solution.py:129
  350.8 1.2 convolution_bitcast_fusion
  (51 shorter events, 4.8 us)
Async XLA Ops:
  6.5 34.5 %copy-start = (bf16[2,1,400,1600]{3,2,1,0:T(8,128)(2,1)S(1)}, bf16[2,1,400,1600]{3,2,1,0:T(8,128)(2,1)}, u32[]{:S(2)}) copy-start(bf16[2,1,400,1600]{3,2,1,0:T(8,128)(2,1)} %param.2) | copy-start | bytes 7680004
  6.5 78.1 %all-reduce.4.cloned.1.call-start = ((), (), s32[]{:S(2)}) async-start(), calls=%async_computation.2 | async-start | bytes 425984 | tf_op jit(solution)/shard_map/psum | solution.py:136
  42.2 99.2 %all-reduce.6.cloned.1.call-start = ((), (), s32[]{:S(2)}) async-start(), calls=%async_computation.3 | async-start | bytes 425984 | tf_op jit(solution)/shard_map/psum | solution.py:136
  87.3 1.6 copy-start.3
  88.9 109.3 %all-reduce.8.cloned.1.call-start = ((), (), s32[]{:S(2)}) async-start(), calls=%async_computation.4 | async-start | bytes 425984 | tf_op jit(solution)/shard_map/psum | solution.py:136
  144.1 1.6 copy-start.1
  198.1 2.1 copy-start.2
Sparse Core Ops, SparseCore 0:
  42.3 42.2 all-reduce.3
  89.0 52.3 all-reduce.5
  145.8 52.3 all-reduce.7
where the time goes:
time: 359 us; the launch traced here: 358 us
  blocking collectives  152 us (42%)
  waiting for transfers between devices  143 us (40%)
  between operations  34.6 us (10%)
  other arithmetic  14.6 us (4%)
  matrix products  9.22 us (3%)
  local copies, waits for them, and re-layouts  5.31 us (1%)
    psum x3, waiting for transfers between devices, on_device(): model = lax.psum(adjoint_product(rows, wave), 'panel')  143 us
    psum x1, blocking collectives, on_device(): squares = lax.psum(jnp.stack(squares), ('freq', 'panel'))  99.4 us
    all_to_all x2, blocking collectives, exchange(): lax.all_to_all(lines, 'freq', split_axis=0, concat_axis=0, tiled=True)  52.3 us
  transfers between devices with their start and end apart: 3, of which 3 were waited for; matrix products, arithmetic and copies ran while one was open for 1% of the time, Pallas kernels for 0%

commit v1 on v0

--- a/solution.py
+++ b/solution.py
@@ -133,7 +133,7 @@
     rows = moved_in.transpose(1, 0, 2).reshape(2 * VS, panel_rows)
     bases, squares = ([], [jnp.sum(data * data)])
     for step in range(ITERS):
-        model = lax.psum(adjoint_product(rows, wave), "panel")
+        model = jnp.sum(lax.all_gather(adjoint_product(rows, wave), "panel"), axis=0)
         image = forward_product(model, wave)
         bases.append(model)
         squares += [jnp.sum(model * model) / panels, jnp.sum(image * image)]

time: 359 us -> 236 us (0.66)
  waiting for transfers between devices: 143 us -> 9.87 us
  starting transfers between devices: 0.09 us -> 18.4 us
  between operations: 34.6 us -> 21.2 us
  blocking collectives: 152 us -> 156 us
    psum x3 -> x0, waiting for transfers between devices: 143 us -> none  [on_device(): model = lax.psum(adjoint_product(rows, wave), 'panel')]
    all_gather x0 -> x3, blocking collectives: none -> 34 us  [on_device(): lax.all_gather(adjoint_product(rows, wave), 'panel')]
    all_to_all x2 -> x1, blocking collectives: 52.3 us -> 19.9 us  [exchange(): lax.all_to_all(lines, 'freq', split_axis=0, concat_axis=0, tiled=True)]
    all_to_all x0 -> x1, starting transfers between devices: none -> 18.4 us  [exchange(): lax.all_to_all(lines, 'freq', split_axis=0, concat_axis=0, tiled=True)]
    all_to_all x0 -> x1, waiting for transfers between devices: none -> 9.87 us  [exchange(): lax.all_to_all(lines, 'freq', split_axis=0, concat_axis=0, tiled=True)]
  transfers between devices with their start and end apart: 3 -> 1, of which waited for: 3 -> 1; matrix products, arithmetic and copies ran while one was open for 1% -> 1% of each run, Pallas kernels for 0% -> 0%
where the time goes in v1:
time: 236 us; the launch traced here: 235 us
  blocking collectives  156 us (66%)
  between operations  21.2 us (9%)
  starting transfers between devices  18.4 us (8%)
  other arithmetic  13.8 us (6%)
  waiting for transfers between devices  9.87 us (4%)
  matrix products  9.21 us (4%)
  local copies, waits for them, and re-layouts  6.84 us (3%)
    psum x1, blocking collectives, on_device(): squares = lax.psum(jnp.stack(squares), ('freq', 'panel'))  102 us
    all_gather x3, blocking collectives, on_device(): lax.all_gather(adjoint_product(rows, wave), 'panel')  34 us
    all_to_all x1, blocking collectives, exchange(): lax.all_to_all(lines, 'freq', split_axis=0, concat_axis=0, tiled=True)  19.9 us
    all_to_all x1, starting transfers between devices, exchange(): lax.all_to_all(lines, 'freq', split_axis=0, concat_axis=0, tiled=True)  18.4 us
    all_to_all x1, waiting for transfers between devices, exchange(): lax.all_to_all(lines, 'freq', split_axis=0, concat_axis=0, tiled=True)  9.87 us
  transfers between devices with their start and end apart: 1, of which 1 were waited for; matrix products, arithmetic and copies ran while one was open for 1% of the time, Pallas kernels for 0%

profile of v1, /device:TPU:1, one launch (start us, length us, event | category | flops | bytes accessed | tf_op | source)
XLA Modules:
  0.0 235.2 jit_solution(12847054690980564816)
XLA Ops:
  0.0 1.1 cosine_multiply_fusion
  1.1 0.7 copy-done.4
  1.9 1.5 fusion.24
  3.4 0.7 copy.6
  4.2 18.4 %all-to-all-start = ((bf16[128,100,1]{1,2,0:T(2,128)(2,1)}), bf16[128,100,1]{1,2,0:T(2,128)(2,1)S(1)}, u32[]{:S(2)}, u32[]{:S(2)}) async-start(bf16[128,100,1]{1,2,0:T(2,128)(2,1)} %copy.6), calls=%async_computation | async-start | bytes 131072 | tf_op jit(solution)/shard_map/all_to_all | solution.py:129
  22.6 1.6 fusion.47
  24.2 9.9 %all-to-all-done = bf16[128,100,1]{1,2,0:T(2,128)(2,1)S(1)} async-done(((bf16[128,100,1]{1,2,0:T(2,128)(2,1)}), bf16[128,100,1]{1,2,0:T(2,128)(2,1)S(1)}, u32[]{:S(2)}, u32[]{:S(2)}) %all-to-all-start) | async-done | bytes 25632 | tf_op jit(solution)/shard_map/all_to_all | solution.py:129
  34.4 1.7 fusion.10
  36.5 12.3 %all_gather.12 = f32[4,2,16,1600]{3,2,1,0:T(8,128)S(1)} all-gather(f32[1,2,16,1600]{3,2,1,0:T(8,128)S(1)} %maximum_multiply_fusion), channel_id=1, replica_groups=mesh['freq'=128,'panel'=4] {'panel'}, dimensions={0}, use_global_device_ids=true | all-gather | bytes 1024000 | tf_op jit(solution)/shard_map/all_gather | solution.py:136
  48.8 0.7 reduce_sum.91
  49.5 1.0 reduce-precision_convert_fusion.2
  51.6 0.6 multiply_reduce_fusion.4
  53.1 10.6 %all_gather.13 = f32[4,2,16,1600]{3,2,1,0:T(8,128)S(1)} all-gather(f32[1,2,16,1600]{3,2,1,0:T(8,128)S(1)} %maximum_multiply_fusion.1), channel_id=1, replica_groups=mesh['freq'=128,'panel'=4] {'panel'}, dimensions={0}, use_global_device_ids=true | all-gather | bytes 1024000 | tf_op jit(solution)/shard_map/all_gather | solution.py:136
  63.7 0.7 reduce_sum.94
  64.4 1.0 reduce-precision_convert_fusion.1
  66.5 0.7 multiply_reduce_fusion.3
  68.1 11.1 %all_gather.14 = f32[4,2,16,1600]{3,2,1,0:T(8,128)S(1)} all-gather(f32[1,2,16,1600]{3,2,1,0:T(8,128)S(1)} %maximum_multiply_fusion.2), channel_id=1, replica_groups=mesh['freq'=128,'panel'=4] {'panel'}, dimensions={0}, use_global_device_ids=true | all-gather | bytes 1024000 | tf_op jit(solution)/shard_map/all_gather | solution.py:136
  79.2 0.7 reduce_sum.97
  79.9 1.0 reduce-precision_convert_fusion
  81.0 0.5 fusion.12
  81.5 0.5 fusion
  82.0 0.7 multiply_reduce_fusion
  82.7 0.7 multiply_reduce_fusion.1
  83.4 0.7 multiply_reduce_fusion.2
  86.1 0.7 fusion.58
  86.8 2.6 %stack.109 = f32[7]{0:T(128)S(1)} concatenate(f32[1]{0:T(128)} %bitcast, f32[1]{0:T(128)} %bitcast.7, f32[1]{0:T(128)} %bitcast.11, f32[1]{0:T(128)} %bitcast.15, f32[1]{0:T(128)} %bitcast.19, f32[1]{0:T(128)} %bitcast.23, f32[1]{0:T(128)} %bitcast.27), dimensions={0} | concatenate | bytes 56 | tf_op jit(solution)/shard_map/stack | solution.py:141
  89.5 102.2 %psum.7 = f32[7]{0:T(128)S(1)} all-reduce(f32[7]{0:T(128)S(1)} %stack.109), channel_id=1, replica_groups=mesh['freq'=128,'panel'=4] {'freq','panel'}, use_global_device_ids=true, to_apply=%region_10.11 | all-reduce | flops 7 | bytes 56 | tf_op jit(solution)/shard_map/psum | solution.py:141
  191.6 0.7 fusion.77
  211.7 0.6 broadcast.172
  212.3 1.4 reduce
  213.9 19.9 %all_to_all.18 = bf16[128,2,200]{2,1,0:T(2,128)(2,1)S(1)} all-to-all(bf16[128,2,200]{2,1,0:T(2,128)(2,1)S(1)} %reshape.246), channel_id=1, replica_groups=mesh['freq'=128,'panel'=4] {'freq'}, dimensions={0} | all-to-all | bytes 204800 | tf_op jit(solution)/shard_map/all_to_all | solution.py:129
  234.1 1.1 convolution_bitcast_fusion
  (57 shorter events, 5.8 us)
Async XLA Ops:
  0.0 36.1 %copy-start = (bf16[2,1,400,1600]{3,2,1,0:T(8,128)(2,1)S(1)}, bf16[2,1,400,1600]{3,2,1,0:T(8,128)(2,1)}, u32[]{:S(2)}) copy-start(bf16[2,1,400,1600]{3,2,1,0:T(8,128)(2,1)} %param.2) | copy-start | bytes 7680004
  1.1 0.7 copy-start.4
  1.1 0.8 copy-start.6
  4.2 29.9 %all-to-all-start = ((bf16[128,100,1]{1,2,0:T(2,128)(2,1)}), bf16[128,100,1]{1,2,0:T(2,128)(2,1)S(1)}, u32[]{:S(2)}, u32[]{:S(2)}) async-start(bf16[128,100,1]{1,2,0:T(2,128)(2,1)} %copy.6), calls=%async_computation | async-start | bytes 131072 | tf_op jit(solution)/shard_map/all_to_all | solution.py:129
  79.9 2.1 copy-start.3
  79.9 2.8 %copy-start.2 = (f32[2,16,1600]{2,1,0:T(8,128)S(1)}, f32[2,16,1600]{2,1,0:T(8,128)}, u32[]{:S(2)}) copy-start(f32[2,16,1600]{2,1,0:T(8,128)} %reduce_sum.94) | copy-start | bytes 614404
  79.9 3.5 %copy-start.1 = (f32[2,16,1600]{2,1,0:T(8,128)S(1)}, f32[2,16,1600]{2,1,0:T(8,128)}, u32[]{:S(2)}) copy-start(f32[2,16,1600]{2,1,0:T(8,128)} %reduce_sum.91) | copy-start | bytes 614404
  82.7 151.4 %copy-start.5 = (f32[1,128,512]{2,1,0:T(8,128)S(1)}, f32[1,128,512]{2,1,0:T(8,128)}, u32[]{:S(2)}) copy-start(f32[1,128,512]{2,1,0:T(8,128)} %copy-done.4) | copy-start | bytes 786436
  82.7 151.4 %copy-start.7 = (f32[1,128,512]{2,1,0:T(8,128)S(1)}, f32[1,128,512]{2,1,0:T(8,128)}, u32[]{:S(2)}) copy-start(f32[1,128,512]{2,1,0:T(8,128)} %copy-done.6) | copy-start | bytes 786436
